TPU v7x, 32 devices: a whole 2x2x4 slice. The times are simulated.
32 devices in a mesh: grp: 2 (over x), rows: 16 (over z, y, core).
Axes of the slice: x: 2, y: 2, z: 4, core: 2. Of those that a mesh axis runs over, the one named last changes fastest.
Arguments:
- histories: float32 [4096, 384], P(('grp', 'rows')), parts along dimension 0, may hold values from -6 to 6
- modal_map: float32 [4096, 8192], P(('grp', 'rows')), parts along dimension 0, may hold values from -0.1875 to 0.1875
- recovery: float32 [8192, 8192], P(('grp', 'rows')), parts along dimension 0, may hold values from -0.0625 to 0.0625
Outputs:
- responses: float32 [8192, 384], P(('grp', 'rows')), parts along dimension 0
- peak_response: float32 [4, 8192], P(None, ('grp', 'rows')), parts along dimension 1
- rms_response: float32 [4, 8192], P(None, ('grp', 'rows')), parts along dimension 1
There are 2 independent parts, one for each index of `grp`. A program takes and returns all parts, laid end to end along the dimension named above; each array names one. Nothing has to cross between parts.
All inputs are finite; a program needn't handle non-finite values.
Results may differ from a plain program's by a relative error of at most 0.000071.
Values sent between devices are 32-bit elements; how exact they have to be, the bound alone decides.
A program may use at most 64 MiB of HBM per device.

v0:
```python
import jax
import jax.numpy as jnp
from jax import lax
from jax.sharding import PartitionSpec as P

CASES = 4


epsilon = 1e-06


def shards(histories, modal_map, recovery):
    time_cols = histories.shape[1]
    modal_rows = lax.psum_scatter(
        lax.dot_general(
            modal_map,
            histories,
            (((0,), (0,)), ((), ())),
            precision=lax.Precision.HIGHEST,
            preferred_element_type=jnp.float32,
        ),
        "rows",
        scatter_dimension=0,
        tiled=True,
    )
    responses = jnp.dot(
        recovery,
        lax.all_gather(modal_rows, "rows", axis=0, tiled=True),
        precision=lax.Precision.HIGHEST,
        preferred_element_type=jnp.float32,
    )
    by_case = responses.reshape(responses.shape[0], CASES, time_cols // CASES)
    peak_response = jnp.max(jnp.abs(by_case), axis=2).T
    rms_response = jnp.sqrt(jnp.mean(by_case * by_case, axis=2) + epsilon).T
    return (responses, peak_response, rms_response)


def solution(mesh):
    return jax.shard_map(
        shards,
        mesh=mesh,
        in_specs=(P(("grp", "rows"), None), P(("grp", "rows"), None), P(("grp", "rows"), None)),
        out_specs=(P(("grp", "rows"), None), P(None, ("grp", "rows")), P(None, ("grp", "rows"))),
        check_vma=False,
    )
```

profile of v0, /device:TPU:0, one launch (start us, length us, event | category | flops | bytes accessed | tf_op | source)
XLA Modules:
  0.0 294.4 jit_solution(7221013684479145059)
XLA Ops:
  7.2 0.0 copy-start
  7.2 0.0 reduce-scatter.2.cloned.1.call-start
  7.2 0.9 copy-done
  8.1 13.6 %fusion.1 = f32[8192,384]{1,0:T(8,128)} fusion(f32[128,8192]{1,0:T(8,128)} %param.4, f32[128,384]{1,0:T(8,128)S(1)} %copy-done), kind=kOutput, calls=%fused_computation.3 | convolution fusion | flops 4831838208 | bytes 16973824 | tf_op jit(solution)/shard_map/dot_general | solution.py:15
  21.7 0.0 reduce-scatter.2.cloned.1.call-update
  21.7 0.2 all-gather.2.cloned.1.call-start
  21.9 137.2 %reduce-scatter.2.cloned.1.call-done = f32[512,384]{1,0:T(8,128)} async-done(((f32[8192,384]{1,0:T(8,128)}), f32[512,384]{1,0:T(8,128)}) %reduce-scatter.2.cloned.1.call-update) | async-done | bytes 786448 | tf_op jit(solution)/shard_map/reduce_scatter | solution.py:14
  159.2 0.0 all-gather.2.cloned.1.call-update
  159.2 102.2 %all-gather.2.cloned.1.call-done = f32[8192,384]{1,0:T(8,128)} async-done(((f32[512,384]{1,0:T(8,128)}), f32[8192,384]{1,0:T(8,128)}) %all-gather.2.cloned.1.call-update) | async-done | bytes 12582928 | tf_op jit(solution)/shard_map/all_gather | solution.py:28
  261.4 23.9 %fusion = (f32[256,384]{0,1:T(8,128)S(1)}, f32[256,384]{0,1:T(8,128)S(1)}, f32[256,384]{0,1:T(8,128)S(1)}) fusion(f32[8192,384]{1,0:T(8,128)} %all-gather.2.cloned.1.call-done, f32[256,8192]{1,0:T(8,128)} %param.5), kind=kOutput, calls=%fused_computation.2 | convolution fusion | flops 9663873024 | bytes 22151168 | tf_op jit(solution)/shard_map/dot_general | solution.py:26
  285.4 0.6 sqrt_bitcast_fusion
  286.0 0.9 copy.6
  286.9 0.6 reduce_max.9
  (1 shorter events, 0.0 us)
Async XLA Ops:
  7.2 0.9 copy-start
  7.2 152.0 %reduce-scatter.2.cloned.1.call-start = ((), (), s32[]{:S(2)}) async-start(), calls=%async_computation.1 | async-start | bytes 13369344 | tf_op jit(solution)/shard_map/reduce_scatter | solution.py:14
  21.7 239.7 %all-gather.2.cloned.1.call-start = ((), (), s32[]{:S(2)}) async-start(), calls=%async_computation.2 | async-start | bytes 13369344 | tf_op jit(solution)/shard_map/all_gather | solution.py:28
Sparse Core Ops, SparseCore 0:
  21.8 137.3 reduce-scatter.1
  161.5 99.8 all-gather.1
where the time goes:
time: 295 us; the launch traced here: 294 us
  waiting for transfers between devices  239 us (81%)
  matrix products  37.5 us (13%)
  between operations  14.1 us (5%)
    reduce_scatter x1, waiting for transfers between devices, shards(): lax.psum_scatter(lax.dot_general(modal_map, histories, (((0,), (0,)), (()...  137 us
    all_gather x1, waiting for transfers between devices, shards(): lax.all_gather(modal_rows, 'rows', axis=0, tiled=True)  102 us
    dot_general x1, matrix products, shards(): jnp.dot(recovery, lax.all_gather(modal_rows, 'rows', axis=0, tiled=True),...  23.9 us
    dot_general x1, matrix products, shards(): lax.dot_general(modal_map, histories, (((0,), (0,)), ((), ())), precision...  13.6 us
  transfers between devices with their start and end apart: 2, of which 2 were waited for; matrix products, arithmetic and copies ran while one was open for 0% of the time, Pallas kernels for 0%

commit v1 on v0

v1 whole, which is shorter than its diff:
```python
import functools

import jax
import jax.numpy as jnp
from jax import lax
from jax.experimental import pallas as pl
from jax.experimental.pallas import tpu as pltpu
from jax.sharding import PartitionSpec as P

CASES = 4
SUBS = 2
epsilon = 1e-06
MESH = pl.DeviceIdType.MESH


def split(x):
    high = x.astype(jnp.bfloat16)
    return high, (x - high.astype(jnp.float32)).astype(jnp.bfloat16)


def dot3(a, b, dims):
    mul = functools.partial(
        lax.dot_general, dimension_numbers=(dims, ((), ())), preferred_element_type=jnp.float32
    )
    return mul(a[0], b[0]) + (mul(a[0], b[1]) + mul(a[1], b[0]))


def ring_position(chips, chip):
    if chips == 8:
        z, y = chip // 2, chip % 2
        return y * (chips - 1 - 2 * z) + z
    return chip


def chip_at(chips, position):
    if chips == 8:
        y = position // 4
        return (y * (chips - 1 - 2 * position) + position) * 2 + y
    return position


def kernel(
    chips, ways, h_ref, m_ref, r_ref, out_ref, peak_ref, rms_ref,
    h_other, hist_hi, hist_lo, m_buf, r_buf, part, landed, rows, acc, acc_other,
    local_sem, pair_send, pair_recv, m_send, m_recv, rs_send, rs_recv, ag_send, ag_recv,
):
    me = lax.axis_index("rows")
    core = me % 2
    partner = me + 1 - 2 * core
    pos = ring_position(chips, me // 2)
    after = chip_at(chips, (pos + 1) % chips) * 2 + core
    before = chip_at(chips, (pos + chips - 1) % chips) * 2 + core
    targets = (after, before)
    signs = (1, -1)

    modes, outs = h_ref.shape[0], r_ref.shape[0]
    half = m_ref.shape[1] // 2
    block = half // chips
    unit = block // ways
    piece = unit // SUBS

    def at(p):
        return (p + 2 * chips) % chips

    def cols(base, b, d):
        return pl.ds(pl.multiple_of(base + b * block + d * unit, 128), unit)

    def remote(src, dst, send, recv, to):
        return pltpu.make_async_remote_copy(
            src_ref=src, dst_ref=dst, send_sem=send, recv_sem=recv,
            device_id={"rows": to}, device_id_type=MESH,
        )

    def sum_block(k, d):
        return at(pos - signs[d] * (k + 1))

    def m_copy(k, d):
        b = sum_block(k, d)
        return remote(
            m_ref.at[:, cols((1 - core) * half, b, d)],
            m_buf.at[pl.ds(modes, modes), cols(0, b, d)],
            m_send.at[d, k], m_recv.at[d, k], partner,
        )

    def rs_copy(k, d, j):
        view = (d, k, pl.ds(j * piece, piece))
        return remote(part.at[view], landed.at[view], rs_send.at[d, k, j], rs_recv.at[d, k, j], targets[d])

    def ag_copy(s, d, j, arrives=False):
        b = at(pos - signs[d] * (s + 1 if arrives else s))
        view = (b, d, pl.ds(j * piece, piece))
        return remote(rows.at[view], rows.at[view], ag_send.at[d, s, j], ag_recv.at[d, s, j], targets[d])

    own_m = pltpu.make_async_copy(
        m_ref.at[:, pl.ds(pl.multiple_of(core * half, 128), half)],
        m_buf.at[pl.ds(0, modes)], local_sem.at[0],
    )
    own_r = pltpu.make_async_copy(
        r_ref.at[:, pl.ds(pl.multiple_of(core * half, 128), half)],
        r_buf.at[pl.ds(0, outs)], local_sem.at[1],
    )
    h_copy = remote(h_ref, h_other, pair_send.at[0], pair_recv.at[0], partner)
    r_copy = remote(
        r_ref.at[:, pl.ds(pl.multiple_of((1 - core) * half, 128), half)],
        r_buf.at[pl.ds(outs, outs)], pair_send.at[1], pair_recv.at[1], partner,
    )
    acc_copy = remote(acc.at[pl.ds(outs, outs)], acc_other, pair_send.at[2], pair_recv.at[2], partner)

    own_m.start()
    own_r.start()
    barrier = pltpu.get_barrier_semaphore()
    for other in (after, before, partner):
        pl.semaphore_signal(barrier, inc=1, device_id={"rows": other}, device_id_type=MESH)
    pl.semaphore_wait(barrier, 3)

    h_copy.start()

    @pl.loop(0, chips)
    def _(k):
        for d in range(ways):
            m_copy(k, d).start()

    r_copy.start()
    own_m.wait()
    h_copy.wait_recv()
    for src, base in ((h_ref, 0), (h_other, modes)):
        hist_hi[pl.ds(base, modes)], hist_lo[pl.ds(base, modes)] = split(src[...])

    def partial_rows(k, d):
        m_copy(k, d).wait_recv()
        shapes = split(m_buf[:, cols(0, sum_block(k, d), d)])
        return dot3(shapes, (hist_hi[...], hist_lo[...]), ((0,), (0,)))

    for d in range(ways):
        part[d, 0] = partial_rows(0, d)
        for j in range(SUBS):
            rs_copy(0, d, j).start()

    @pl.loop(1, chips - 1)
    def _(k):
        for d in range(ways):
            part[d, k] = partial_rows(k, d)
        for j in range(SUBS):
            for d in range(ways):
                rs_copy(k - 1, d, j).wait_recv()
                view = (d, k, pl.ds(j * piece, piece))
                part[view] = part[view] + landed[d, k - 1, pl.ds(j * piece, piece)]
                rs_copy(k, d, j).start()

    last = chips - 1
    for d in range(ways):
        rows[pos, d] = partial_rows(last, d)
    for j in range(SUBS):
        for d in range(ways):
            rs_copy(last - 1, d, j).wait_recv()
            view = (pos, d, pl.ds(j * piece, piece))
            rows[view] = rows[view] + landed[d, last - 1, pl.ds(j * piece, piece)]
            ag_copy(0, d, j).start()

    own_r.wait()
    r_copy.wait_recv()

    def recovered(b, d):
        return dot3(split(r_buf[:, cols(0, b, d)]), split(rows[b, d]), ((1,), (0,)))

    acc[...] = recovered(pos, 0)
    for d in range(1, ways):
        acc[...] += recovered(pos, d)

    @pl.loop(0, chips - 2)
    def _(s):
        for j in range(SUBS):
            for d in range(ways):
                ag_copy(s, d, j, arrives=True).wait_recv()
                ag_copy(s + 1, d, j).start()
        for d in range(ways):
            acc[...] += recovered(at(pos - signs[d] * (s + 1)), d)

    for d in range(ways):
        for j in range(SUBS):
            ag_copy(chips - 2, d, j, arrives=True).wait_recv()
        acc[...] += recovered(at(pos - signs[d] * (chips - 1)), d)

    acc_copy.start()

    h_copy.wait_send()
    r_copy.wait_send()

    @pl.loop(0, chips)
    def _(k):
        for d in range(ways):
            m_copy(k, d).wait_send()

    @pl.loop(0, chips - 1)
    def _(k):
        for d in range(ways):
            for j in range(SUBS):
                rs_copy(k, d, j).wait_send()
                ag_copy(k, d, j).wait_send()

    acc_copy.wait()
    responses = acc[pl.ds(0, outs)] + acc_other[...]
    out_ref[...] = responses
    by_time = responses.T
    steps = by_time.shape[0] // CASES
    for k in range(CASES):
        case = by_time[k * steps : (k + 1) * steps]
        peak_ref[k : k + 1] = jnp.max(jnp.abs(case), axis=0, keepdims=True)
        mean = jnp.sum(case * case, axis=0, keepdims=True) / steps
        rms_ref[k : k + 1] = jnp.sqrt(mean + epsilon)


def shards(size, histories, modal_map, recovery):
    chips = size // 2
    modes, time_cols = histories.shape
    outs, dofs = recovery.shape
    half = dofs // 2
    block = half // chips
    ways = 2 if block % 256 == 0 else 1
    unit = block // ways
    f32, dma = jnp.float32, pltpu.SemaphoreType.DMA
    vmem, anywhere = pl.BlockSpec(memory_space=pltpu.VMEM), pl.BlockSpec(memory_space=pl.ANY)
    return pl.pallas_call(
        functools.partial(kernel, chips, ways),
        out_shape=(
            jax.ShapeDtypeStruct((outs, time_cols), f32),
            jax.ShapeDtypeStruct((CASES, outs), f32),
            jax.ShapeDtypeStruct((CASES, outs), f32),
        ),
        in_specs=[vmem, anywhere, anywhere],
        out_specs=(vmem, vmem, vmem),
        scratch_shapes=[
            pltpu.VMEM((modes, time_cols), f32),
            pltpu.VMEM((2 * modes, time_cols), jnp.bfloat16),
            pltpu.VMEM((2 * modes, time_cols), jnp.bfloat16),
            pltpu.VMEM((2 * modes, half), f32),
            pltpu.VMEM((2 * outs, half), f32),
            pltpu.VMEM((ways, chips - 1, unit, time_cols), f32),
            pltpu.VMEM((ways, chips - 1, unit, time_cols), f32),
            pltpu.VMEM((chips, ways, unit, time_cols), f32),
            pltpu.VMEM((2 * outs, time_cols), f32),
            pltpu.VMEM((outs, time_cols), f32),
            dma((2,)),
            dma((3,)),
            dma((3,)),
            dma((ways, chips)),
            dma((ways, chips)),
            dma((ways, chips - 1, SUBS)),
            dma((ways, chips - 1, SUBS)),
            dma((ways, chips - 1, SUBS)),
            dma((ways, chips - 1, SUBS)),
        ],
        compiler_params=pltpu.CompilerParams(
            collective_id=0, has_side_effects=True, vmem_limit_bytes=50 * 2**20
        ),
    )(histories, modal_map, recovery)


def solution(mesh):
    return jax.shard_map(
        functools.partial(shards, mesh.shape["rows"]),
        mesh=mesh,
        in_specs=(P(("grp", "rows"), None), P(("grp", "rows"), None), P(("grp", "rows"), None)),
        out_specs=(P(("grp", "rows"), None), P(None, ("grp", "rows")), P(None, ("grp", "rows"))),
        check_vma=False,
    )
```

time: 295 us -> 133 us (0.45)
  waiting for transfers between devices: 239 us -> 0 us
  Pallas kernels: 0 us -> 129 us
  matrix products: 37.5 us -> 0 us
  between operations: 14.1 us -> 0.65 us
    reduce_scatter x1 -> x0, waiting for transfers between devices: 137 us -> none  [shards(): lax.psum_scatter(lax.dot_general(modal_map, histories, (((0,), (0,)), (()...]
    pallas_call x0 -> x1, Pallas kernels: none -> 129 us  [shards(): pl.pallas_call(functools.partial(kernel, chips, ways), out_shape=(jax.Sha...]
    all_gather x1 -> x0, waiting for transfers between devices: 102 us -> none  [shards(): lax.all_gather(modal_rows, 'rows', axis=0, tiled=True)]
    dot_general x2 -> x0, matrix products: 37.5 us -> none  [the longest x1 23.9 us: shards(): jnp.dot(recovery, lax.all_gather(modal_rows, 'rows', axis=0, tiled=True),...]
  transfers between devices with their start and end apart: 2 -> 0, of which waited for: 2 -> 0; matrix products, arithmetic and copies ran while one was open for 0% -> 0% of each run, Pallas kernels for 0% -> 0%
where the time goes in v1:
time: 133 us
  Pallas kernels  129 us (97%)
  local copies, waits for them, and re-layouts  2.85 us (2%)
    pallas_call x1, Pallas kernels, shards(): pl.pallas_call(functools.partial(kernel, chips, ways), out_shape=(jax.Sha...  129 us
    unnamed x5, local copies, waits for them, and re-layouts  2.85 us

profile of v1, /device:TPU:0, one launch (start us, length us, event | category | flops | bytes accessed | tf_op | source)
XLA Modules:
  0.0 132.7 jit_solution(5447194596664580698)
XLA Ops:
  0.6 0.0 copy-start
  0.6 0.9 copy-done
  1.6 129.2 %shard_map.58 = (f32[256,384]{1,0:T(8,128)S(1)}, f32[4,256]{1,0:T(4,128)S(1)}, f32[4,256]{1,0:T(4,128)S(1)}) custom-call(f32[128,384]{1,0:T(8,128)S(1)} %copy-done, f32[128,8192]{1,0:T(8,128)} %m_ref.1, f32[256,8192]{1,0:T(8,128)} %r_ref.1), custom_call_target="tpu_custom_call" | custom-call | tf_op jit(solution)/shard_map/pallas_call | solution.py:223
  130.8 0.7 copy.9
  131.5 0.6 copy.10
  132.1 0.6 copy.11
Async XLA Ops:
  0.6 0.9 copy-start

commit v2 on v1

--- a/solution.py
+++ b/solution.py
@@ -40,9 +40,9 @@
 
 
 def kernel(
-    chips, ways, h_ref, m_ref, r_ref, out_ref, peak_ref, rms_ref,
-    h_other, hist_hi, hist_lo, m_buf, r_buf, part, landed, rows, acc, acc_other,
-    local_sem, pair_send, pair_recv, m_send, m_recv, rs_send, rs_recv, ag_send, ag_recv,
+    chips, ways, h_ref, m_ref, r_ref, out_ref,
+    hist, hist_hi, hist_lo, m_buf, r_buf, part, landed, rows, acc, acc_other,
+    local_sem, pair_send, pair_recv, m_local, m_send, m_recv, rs_send, rs_recv, ag_send, ag_recv,
 ):
     me = lax.axis_index("rows")
     core = me % 2
@@ -58,12 +58,14 @@
     block = half // chips
     unit = block // ways
     piece = unit // SUBS
+    cuts = SUBS if piece % 128 == 0 else 1
+    width = unit // cuts
 
     def at(p):
         return (p + 2 * chips) % chips
 
-    def cols(base, b, d):
-        return pl.ds(pl.multiple_of(base + b * block + d * unit, 128), unit)
+    def cols(base, b, d, start=0, size=unit):
+        return pl.ds(pl.multiple_of(base + b * block + d * unit + start, 128), size)
 
     def remote(src, dst, send, recv, to):
         return pltpu.make_async_remote_copy(
@@ -82,6 +84,13 @@
             m_send.at[d, k], m_recv.at[d, k], partner,
         )
 
+    def own_m(k, d):
+        b = sum_block(k, d)
+        return pltpu.make_async_copy(
+            m_ref.at[:, cols(core * half, b, d)],
+            m_buf.at[pl.ds(0, modes), cols(0, b, d)], m_local.at[d, k],
+        )
+
     def rs_copy(k, d, j):
         view = (d, k, pl.ds(j * piece, piece))
         return remote(part.at[view], landed.at[view], rs_send.at[d, k, j], rs_recv.at[d, k, j], targets[d])
@@ -91,54 +100,65 @@
         view = (b, d, pl.ds(j * piece, piece))
         return remote(rows.at[view], rows.at[view], ag_send.at[d, s, j], ag_recv.at[d, s, j], targets[d])
 
-    own_m = pltpu.make_async_copy(
-        m_ref.at[:, pl.ds(pl.multiple_of(core * half, 128), half)],
-        m_buf.at[pl.ds(0, modes)], local_sem.at[0],
-    )
+    own_h = pltpu.make_async_copy(h_ref, hist.at[pl.ds(0, modes)], local_sem.at[0])
     own_r = pltpu.make_async_copy(
         r_ref.at[:, pl.ds(pl.multiple_of(core * half, 128), half)],
         r_buf.at[pl.ds(0, outs)], local_sem.at[1],
     )
-    h_copy = remote(h_ref, h_other, pair_send.at[0], pair_recv.at[0], partner)
+    h_copy = remote(h_ref, hist.at[pl.ds(modes, modes)], pair_send.at[0], pair_recv.at[0], partner)
     r_copy = remote(
         r_ref.at[:, pl.ds(pl.multiple_of((1 - core) * half, 128), half)],
         r_buf.at[pl.ds(outs, outs)], pair_send.at[1], pair_recv.at[1], partner,
     )
     acc_copy = remote(acc.at[pl.ds(outs, outs)], acc_other, pair_send.at[2], pair_recv.at[2], partner)
 
-    own_m.start()
-    own_r.start()
+    own_h.start()
+    for d in range(ways):
+        own_m(0, d).start()
     barrier = pltpu.get_barrier_semaphore()
     for other in (after, before, partner):
         pl.semaphore_signal(barrier, inc=1, device_id={"rows": other}, device_id_type=MESH)
     pl.semaphore_wait(barrier, 3)
 
     h_copy.start()
-
-    @pl.loop(0, chips)
+    for d in range(ways):
+        m_copy(0, d).start()
+
+    @pl.loop(1, chips)
     def _(k):
         for d in range(ways):
+            own_m(k, d).start()
             m_copy(k, d).start()
 
+    own_h.wait()
+    hist_hi[pl.ds(0, modes)], hist_lo[pl.ds(0, modes)] = split(hist[pl.ds(0, modes)])
+    h_copy.wait_recv()
+    hist_hi[pl.ds(modes, modes)], hist_lo[pl.ds(modes, modes)] = split(hist[pl.ds(modes, modes)])
+
+    def shapes_here(k, d):
+        own_m(k, d).wait()
+        m_copy(k, d).wait_recv()
+
+    def partial_rows(k, d, start=0, size=unit):
+        shapes = split(m_buf[:, cols(0, sum_block(k, d), d, start, size)])
+        return dot3(shapes, (hist_hi[...], hist_lo[...]), ((0,), (0,)))
+
+    for cut in range(cuts):
+        for d in range(ways):
+            if cut == 0:
+                shapes_here(0, d)
+            start = cut * width
+            part[d, 0, pl.ds(start, width)] = partial_rows(0, d, start, width)
+            for j in range(cut * SUBS // cuts, (cut + 1) * SUBS // cuts):
+                rs_copy(0, d, j).start()
+
+    own_r.start()
     r_copy.start()
-    own_m.wait()
-    h_copy.wait_recv()
-    for src, base in ((h_ref, 0), (h_other, modes)):
-        hist_hi[pl.ds(base, modes)], hist_lo[pl.ds(base, modes)] = split(src[...])
-
-    def partial_rows(k, d):
-        m_copy(k, d).wait_recv()
-        shapes = split(m_buf[:, cols(0, sum_block(k, d), d)])
-        return dot3(shapes, (hist_hi[...], hist_lo[...]), ((0,), (0,)))
-
-    for d in range(ways):
-        part[d, 0] = partial_rows(0, d)
-        for j in range(SUBS):
-            rs_copy(0, d, j).start()
 
     @pl.loop(1, chips - 1)
     def _(k):
         for d in range(ways):
+            shapes_here(k, d)
             part[d, k] = partial_rows(k, d)
         for j in range(SUBS):
             for d in range(ways):
@@ -149,6 +169,7 @@
 
     last = chips - 1
     for d in range(ways):
+        shapes_here(last, d)
         rows[pos, d] = partial_rows(last, d)
     for j in range(SUBS):
         for d in range(ways):
@@ -176,12 +197,19 @@
         for d in range(ways):
             acc[...] += recovered(at(pos - signs[d] * (s + 1)), d)
 
-    for d in range(ways):
-        for j in range(SUBS):
-            ag_copy(chips - 2, d, j, arrives=True).wait_recv()
-        acc[...] += recovered(at(pos - signs[d] * (chips - 1)), d)
-
-    acc_copy.start()
+    for cut in range(cuts):
+        for d in range(ways):
+            for j in range(cut * SUBS // cuts, (cut + 1) * SUBS // cuts):
+                ag_copy(chips - 2, d, j, arrives=True).wait_recv()
+            b, start = at(pos - signs[d] * (chips - 1)), cut * width
+            weights = split(r_buf[:, cols(0, b, d, start, width)])
+            finished = split(rows[b, d, pl.ds(start, width)])
+            final = cut == cuts - 1 and d == ways - 1
+            for base in (outs, 0):
+                own = tuple(w[base : base + outs] for w in weights)
+                acc[pl.ds(base, outs)] += dot3(own, finished, ((1,), (0,)))
+                if final and base:
+                    acc_copy.start()
 
     h_copy.wait_send()
     r_copy.wait_send()
@@ -199,7 +227,11 @@
                 ag_copy(k, d, j).wait_send()
 
     acc_copy.wait()
-    responses = acc[pl.ds(0, outs)] + acc_other[...]
+    out_ref[...] = acc[pl.ds(0, outs)] + acc_other[...]
+
+
+def statistics(found_ref, out_ref, peak_ref, rms_ref):
+    responses = found_ref[...]
     out_ref[...] = responses
     by_time = responses.T
     steps = by_time.shape[0] // CASES
@@ -219,18 +251,14 @@
     ways = 2 if block % 256 == 0 else 1
     unit = block // ways
     f32, dma = jnp.float32, pltpu.SemaphoreType.DMA
-    vmem, anywhere = pl.BlockSpec(memory_space=pltpu.VMEM), pl.BlockSpec(memory_space=pl.ANY)
-    return pl.pallas_call(
+    vmem, anywhere = pl.BlockSpec(memory_space=pltpu.VMEM), pl.BlockSpec(memory_space=pltpu.HBM)
+    found = pl.pallas_call(
         functools.partial(kernel, chips, ways),
-        out_shape=(
-            jax.ShapeDtypeStruct((outs, time_cols), f32),
-            jax.ShapeDtypeStruct((CASES, outs), f32),
-            jax.ShapeDtypeStruct((CASES, outs), f32),
-        ),
-        in_specs=[vmem, anywhere, anywhere],
-        out_specs=(vmem, vmem, vmem),
+        out_shape=jax.ShapeDtypeStruct((outs, time_cols), f32),
+        in_specs=[anywhere, anywhere, anywhere],
+        out_specs=vmem,
         scratch_shapes=[
-            pltpu.VMEM((modes, time_cols), f32),
+            pltpu.VMEM((2 * modes, time_cols), f32),
             pltpu.VMEM((2 * modes, time_cols), jnp.bfloat16),
             pltpu.VMEM((2 * modes, time_cols), jnp.bfloat16),
             pltpu.VMEM((2 * modes, half), f32),
@@ -245,6 +273,7 @@
             dma((3,)),
             dma((ways, chips)),
             dma((ways, chips)),
+            dma((ways, chips)),
             dma((ways, chips - 1, SUBS)),
             dma((ways, chips - 1, SUBS)),
             dma((ways, chips - 1, SUBS)),
@@ -254,6 +283,16 @@
             collective_id=0, has_side_effects=True, vmem_limit_bytes=50 * 2**20
         ),
     )(histories, modal_map, recovery)
+    return pl.pallas_call(
+        statistics,
+        out_shape=(
+            jax.ShapeDtypeStruct((outs, time_cols), f32),
+            jax.ShapeDtypeStruct((CASES, outs), f32),
+            jax.ShapeDtypeStruct((CASES, outs), f32),
+        ),
+        in_specs=[vmem], compiler_params=pltpu.CompilerParams(vmem_limit_bytes=8 * 2**20),
+        out_specs=(vmem, vmem, vmem),
+    )(found)
 
 
 def solution(mesh):

time: 133 us -> 132 us (level)
  local copies, waits for them, and re-layouts: 2.85 us -> 0.92 us
    unnamed x5 -> x2, local copies, waits for them, and re-layouts: 2.85 us -> 0.92 us
    pallas_call x1 -> x2, Pallas kernels: 129 us -> 130 us  [the longest x1 129 us: shards(): pl.pallas_call(functools.partial(kernel, chips, ways), out_shape=jax.Shap...]
where the time goes in v2:
time: 132 us
  Pallas kernels  130 us (98%)
    pallas_call x1, Pallas kernels, shards(): pl.pallas_call(functools.partial(kernel, chips, ways), out_shape=jax.Shap...  129 us

profile of v2, /device:TPU:0, one launch (start us, length us, event | category | flops | bytes accessed | tf_op | source)
XLA Modules:
  0.0 131.7 jit_solution(2113194433885192949)
XLA Ops:
  0.6 0.0 copy-start
  0.6 0.9 copy-done
  1.6 129.3 %shard_map.58.found_ref = f32[256,384]{1,0:T(8,128)S(1)} custom-call(f32[128,384]{1,0:T(8,128)S(1)} %copy-done, f32[128,8192]{1,0:T(8,128)} %m_ref.1, f32[256,8192]{1,0:T(8,128)} %r_ref.1), custom_call_target="tpu_custom_call" | custom-call | tf_op jit(solution)/shard_map/pallas_call | solution.py:255
  130.9 0.8 shard_map.59
Async XLA Ops:
  0.6 0.9 copy-start
